TPU v7x, 32 devices: a whole 2x2x4 slice. The times are simulated.
32 devices in a mesh: pipe: 2 (over y), ctx: 16 (over z, x, core).
Axes of the slice: x: 2, y: 2, z: 4, core: 2. Of those that a mesh axis runs over, the one named last changes fastest.
Arguments:
- saved_qkv: bfloat16 [2, 3, 2048, 2048], P('pipe', None, 'ctx'), may hold values from -6 to 6
- handed: bfloat16 [2, 2048, 2048], P('pipe', 'ctx'), may hold values from -6 to 6
- long_filter: bfloat16 [2, 128, 128], P('pipe'), may hold values from -0.5 to 0.5
- short_filter: bfloat16 [2, 3, 3, 2048], P('pipe'), may hold values from -3.5 to 3.5
- doc_lengths: int32 [16], replicated, may hold values from 1 to 512, 2048 in all
Outputs:
- grad_pre: bfloat16 [2, 3, 2048, 2048], P('pipe', None, 'ctx')
- filter_grad: float32 [2, 128, 128], P('pipe')
Inputs may be any that keep to these rules, and one draw needn't show every extreme that they name: `doc_lengths`: documents lie end to end and sum to 2048 tokens; the longest has exactly 512 tokens.
All inputs are finite; a program needn't handle non-finite values.
Results may differ from a plain program's by a relative error of at most 0.0058.
Values may be sent and summed in bfloat16 or wider, within the bound.
A program may use at most 64 MiB of HBM per device.

v0:
```python
import math
import jax
import jax.numpy as jnp
from jax import lax
from jax.sharding import PartitionSpec as P


def from_behind(shard, axis, by):
    count = lax.axis_size(axis)
    return lax.ppermute(shard, axis, [(i, (i + by) % count) for i in range(count)])


def shifted_2(block, axis, distance):
    devices = range(lax.axis_size(axis))
    route = [(i - distance, i) for i in devices if i - distance in devices]
    return lax.ppermute(block, axis, route)


def back_conv(grad_rows, grad_pos, filt, out_len, members, unroll):
    tap_count = filt.shape[0]
    channels = grad_rows.shape[1]

    def step(total, base):
        for offset in range(unroll):
            lag = base * unroll + offset
            ahead = lax.dynamic_slice_in_dim(grad_rows, lag, out_len, 0).astype(jnp.float32)
            ahead_pos = lax.dynamic_slice_in_dim(grad_pos, lag, out_len, 0)
            weights = jnp.repeat(filt[lag].astype(jnp.float32), members)
            total = total + jnp.where((lag <= ahead_pos)[:, None], ahead * weights[None, :], 0.0)
        return (total, None)

    bases = jnp.arange(tap_count // unroll, dtype=jnp.int32)
    result, _ = lax.scan(step, jnp.zeros((out_len, channels), jnp.float32), bases)
    return result


def body(saved_qkv, handed, long_filter, short_filter, doc_lengths):
    query_rows = saved_qkv[0, 0]
    key_rows = saved_qkv[0, 1]
    value_rows = saved_qkv[0, 2]
    filt = long_filter[0]
    tap_count, groups = filt.shape
    row_count, channels = query_rows.shape
    members = channels // groups
    short_taps = short_filter.shape[2]
    unroll = math.gcd(tap_count, 16)
    devices = lax.axis_size("ctx")
    device_index = lax.axis_index("ctx")
    starts = jnp.cumsum(doc_lengths) - doc_lengths
    global_rows = device_index * row_count + jnp.arange(row_count + tap_count, dtype=jnp.int32)
    latest = jnp.max(jnp.where(starts[None, :] <= global_rows[:, None], starts[None, :], 0), axis=1)
    position = global_rows - latest
    own_pos = position[:row_count]
    incoming = from_behind(handed[0], "pipe", -1)
    product = (key_rows.astype(jnp.float32) * value_rows.astype(jnp.float32)).astype(jnp.bfloat16)
    tail_rows = shifted_2(product, "ctx", 1)
    extended = jnp.concatenate([tail_rows, product], axis=0)
    conv_grad = (incoming.astype(jnp.float32) * query_rows.astype(jnp.float32)).astype(jnp.bfloat16)
    grad_wide = conv_grad.astype(jnp.float32)

    def forward_step(total, base):
        columns = []
        for offset in range(unroll):
            lag = base * unroll + offset
            shifted = lax.dynamic_slice_in_dim(extended, tap_count - lag, row_count, 0).astype(
                jnp.float32
            )
            weights = jnp.repeat(filt[lag].astype(jnp.float32), members)
            usable = (lag <= own_pos)[:, None]
            total = total + jnp.where(usable, shifted * weights[None, :], 0.0)
            pair = jnp.sum(
                (grad_wide * shifted).reshape(row_count, groups, members), axis=2
            ).astype(jnp.bfloat16)
            pair = lax.optimization_barrier(pair).astype(jnp.float32)
            columns.append(jnp.sum(jnp.where(usable, pair, 0.0), axis=0))
        return (total, jnp.stack(columns))

    bases = jnp.arange(tap_count // unroll, dtype=jnp.int32)
    conv_out, filter_cols = lax.scan(
        forward_step, jnp.zeros((row_count, channels), jnp.float32), bases
    )
    filter_sum = filter_cols.reshape(tap_count, groups)
    head_rows = shifted_2(conv_grad, "ctx", -1)
    joined = jnp.concatenate([conv_grad, head_rows], axis=0)
    own_grad = back_conv(joined, position, filt, row_count, members, unroll)
    query_grad = (incoming.astype(jnp.float32) * conv_out).astype(jnp.bfloat16)
    key_grad = (own_grad * value_rows.astype(jnp.float32)).astype(jnp.bfloat16)
    value_grad = (own_grad * key_rows.astype(jnp.float32)).astype(jnp.bfloat16)
    stacked = jnp.stack([query_grad, key_grad, value_grad])
    rim_rows = shifted_2(stacked[:, : short_taps - 1], "ctx", -1)
    stacked_ext = jnp.concatenate([stacked, rim_rows], axis=1)
    weights_all = short_filter[0]
    total = jnp.zeros((3, row_count, channels), jnp.float32)
    for shift_by in range(short_taps):
        usable = (shift_by <= position[shift_by : shift_by + row_count])[None, :, None]
        weights = weights_all[:, shift_by].astype(jnp.float32)[:, None, :]
        total = total + jnp.where(
            usable,
            weights * stacked_ext[:, shift_by : shift_by + row_count].astype(jnp.float32),
            0.0,
        )
    grad_pre = total.astype(jnp.bfloat16)[None]
    summed = lax.psum(filter_sum, "ctx")
    filter_grad = (summed / math.sqrt(row_count * devices * members))[None]
    return (grad_pre, filter_grad)


def solution(mesh):
    return jax.shard_map(
        body,
        mesh=mesh,
        in_specs=(
            P("pipe", None, "ctx", None),
            P("pipe", "ctx", None),
            P("pipe", None, None),
            P("pipe", None, None, None),
            P(),
        ),
        out_specs=(P("pipe", None, "ctx", None), P("pipe", None, None)),
        check_vma=False,
    )
```

profile of v0, /device:TPU:8, one launch (start us, length us, event | category | flops | bytes accessed | tf_op | source)
XLA Modules:
  0.0 410.6 jit_solution(385893030262521515)
XLA Ops:
  8.8 12.4 %collective-permute-done = bf16[128,2048]{1,0:T(8,128)(2,1)S(1)} collective-permute-done((bf16[128,2048]{1,0:T(8,128)(2,1)}, bf16[128,2048]{1,0:T(8,128)(2,1)S(1)}, u32[]{:S(2)}, u32[]{:S(2)}) %collective-permute-start) | collective-permute-done | bytes 524320 | tf_op jit(solution)/shard_map/ppermute | solution.py:10
  26.2 5.0 %collective-permute-done.2 = bf16[128,2048]{1,0:T(8,128)(2,1)S(1)} collective-permute-done((bf16[128,2048]{1,0:T(8,128)(2,1)S(1)}, bf16[128,2048]{1,0:T(8,128)(2,1)S(1)}, u32[]{:S(2)}, u32[]{:S(2)}) %collective-permute-start.2) | collective-permute-done | bytes 524320 | tf_op jit(solution)/shard_map/ppermute | solution.py:16
  31.3 81.4 %while.30 = (s32[]{:T(128)}, f32[128,2048]{1,0:T(8,128)S(1)}, s32[8]{0:T(128)S(1)}, s32[256]{0:T(256)S(1)}, bf16[256,2048]{1,0:T(8,128)(2,1)S(1)}, /*index=5*/bf...) while((s32[]{:T(128)}, f32[128,2048]{1,0:T(8,128)S(1)}, ...), condition=%wide.region_37.38_spmd.clone, body=%wide.region_36.37_spmd.clone.sunk | while | flops 17043556 | bytes 11044691 | solution.py:33
  35.9 5.6 %fusion.128 = f32[128,2048]{1,0:T(8,128)S(1)} fusion(f32[128,2048]{1,0:T(8,128)S(1)} %get-tuple-element.835, f32[2048]{0:T(1024)S(1)} %mul.1435, bf16[256,2048]{1,0:T(8,128)(2,1)S(1)} %get-tuple-element.893, s32[]{:T(128)S(6)} %select_n.1196, f32[2048]{0:T(1024)S(1)} %mul.1436, s32[]{:T(128)S(6)} %select_n.1197, f32[2048]{0:T(1024)S(1)} %mul.1437, ...), kind=kLoop, calls=%fused_computation.176.clone.1 | loop fusion | flops 17039360 | bytes 10618945 | tf_op jit(solution)/shard_map/while/body/eval_jaxpr/add | solution.py:29
  46.1 5.6 %fusion.128 = f32[128,2048]{1,0:T(8,128)S(1)} fusion(f32[128,2048]{1,0:T(8,128)S(1)} %get-tuple-element.835, f32[2048]{0:T(1024)S(1)} %mul.1435, bf16[256,2048]{1,0:T(8,128)(2,1)S(1)} %get-tuple-element.893, s32[]{:T(128)S(6)} %select_n.1196, f32[2048]{0:T(1024)S(1)} %mul.1436, s32[]{:T(128)S(6)} %select_n.1197, f32[2048]{0:T(1024)S(1)} %mul.1437, ...), kind=kLoop, calls=%fused_computation.176.clone.1 | loop fusion | flops 17039360 | bytes 10618945 | tf_op jit(solution)/shard_map/while/body/eval_jaxpr/add | solution.py:29
  56.2 5.6 %fusion.128 = f32[128,2048]{1,0:T(8,128)S(1)} fusion(f32[128,2048]{1,0:T(8,128)S(1)} %get-tuple-element.835, f32[2048]{0:T(1024)S(1)} %mul.1435, bf16[256,2048]{1,0:T(8,128)(2,1)S(1)} %get-tuple-element.893, s32[]{:T(128)S(6)} %select_n.1196, f32[2048]{0:T(1024)S(1)} %mul.1436, s32[]{:T(128)S(6)} %select_n.1197, f32[2048]{0:T(1024)S(1)} %mul.1437, ...), kind=kLoop, calls=%fused_computation.176.clone.1 | loop fusion | flops 17039360 | bytes 10618945 | tf_op jit(solution)/shard_map/while/body/eval_jaxpr/add | solution.py:29
  66.4 5.6 %fusion.128 = f32[128,2048]{1,0:T(8,128)S(1)} fusion(f32[128,2048]{1,0:T(8,128)S(1)} %get-tuple-element.835, f32[2048]{0:T(1024)S(1)} %mul.1435, bf16[256,2048]{1,0:T(8,128)(2,1)S(1)} %get-tuple-element.893, s32[]{:T(128)S(6)} %select_n.1196, f32[2048]{0:T(1024)S(1)} %mul.1436, s32[]{:T(128)S(6)} %select_n.1197, f32[2048]{0:T(1024)S(1)} %mul.1437, ...), kind=kLoop, calls=%fused_computation.176.clone.1 | loop fusion | flops 17039360 | bytes 10618945 | tf_op jit(solution)/shard_map/while/body/eval_jaxpr/add | solution.py:29
  76.6 5.6 %fusion.128 = f32[128,2048]{1,0:T(8,128)S(1)} fusion(f32[128,2048]{1,0:T(8,128)S(1)} %get-tuple-element.835, f32[2048]{0:T(1024)S(1)} %mul.1435, bf16[256,2048]{1,0:T(8,128)(2,1)S(1)} %get-tuple-element.893, s32[]{:T(128)S(6)} %select_n.1196, f32[2048]{0:T(1024)S(1)} %mul.1436, s32[]{:T(128)S(6)} %select_n.1197, f32[2048]{0:T(1024)S(1)} %mul.1437, ...), kind=kLoop, calls=%fused_computation.176.clone.1 | loop fusion | flops 17039360 | bytes 10618945 | tf_op jit(solution)/shard_map/while/body/eval_jaxpr/add | solution.py:29
  86.7 5.6 %fusion.128 = f32[128,2048]{1,0:T(8,128)S(1)} fusion(f32[128,2048]{1,0:T(8,128)S(1)} %get-tuple-element.835, f32[2048]{0:T(1024)S(1)} %mul.1435, bf16[256,2048]{1,0:T(8,128)(2,1)S(1)} %get-tuple-element.893, s32[]{:T(128)S(6)} %select_n.1196, f32[2048]{0:T(1024)S(1)} %mul.1436, s32[]{:T(128)S(6)} %select_n.1197, f32[2048]{0:T(1024)S(1)} %mul.1437, ...), kind=kLoop, calls=%fused_computation.176.clone.1 | loop fusion | flops 17039360 | bytes 10618945 | tf_op jit(solution)/shard_map/while/body/eval_jaxpr/add | solution.py:29
  96.9 5.6 %fusion.128 = f32[128,2048]{1,0:T(8,128)S(1)} fusion(f32[128,2048]{1,0:T(8,128)S(1)} %get-tuple-element.835, f32[2048]{0:T(1024)S(1)} %mul.1435, bf16[256,2048]{1,0:T(8,128)(2,1)S(1)} %get-tuple-element.893, s32[]{:T(128)S(6)} %select_n.1196, f32[2048]{0:T(1024)S(1)} %mul.1436, s32[]{:T(128)S(6)} %select_n.1197, f32[2048]{0:T(1024)S(1)} %mul.1437, ...), kind=kLoop, calls=%fused_computation.176.clone.1 | loop fusion | flops 17039360 | bytes 10618945 | tf_op jit(solution)/shard_map/while/body/eval_jaxpr/add | solution.py:29
  107.1 5.6 %fusion.128 = f32[128,2048]{1,0:T(8,128)S(1)} fusion(f32[128,2048]{1,0:T(8,128)S(1)} %get-tuple-element.835, f32[2048]{0:T(1024)S(1)} %mul.1435, bf16[256,2048]{1,0:T(8,128)(2,1)S(1)} %get-tuple-element.893, s32[]{:T(128)S(6)} %select_n.1196, f32[2048]{0:T(1024)S(1)} %mul.1436, s32[]{:T(128)S(6)} %select_n.1197, f32[2048]{0:T(1024)S(1)} %mul.1437, ...), kind=kLoop, calls=%fused_computation.176.clone.1 | loop fusion | flops 17039360 | bytes 10618945 | tf_op jit(solution)/shard_map/while/body/eval_jaxpr/add | solution.py:29
  115.3 3.8 collective-permute-start.1
  119.5 7.5 %collective-permute-done.1 = bf16[128,2048]{1,0:T(8,128)(2,1)} collective-permute-done((bf16[128,2048]{1,0:T(8,128)(2,1)S(1)}, bf16[128,2048]{1,0:T(8,128)(2,1)}, u32[]{:S(2)}, u32[]{:S(2)}) %collective-permute-start.1) | collective-permute-done | bytes 524320 | tf_op jit(solution)/shard_map/ppermute | solution.py:16
  130.6 178.6 %while.29 = (s32[]{:T(128)}, f32[128,2048]{0,1:T(8,128)S(1)}, f32[8,16,128]{2,1,0:T(8,128)}, s32[8]{0:T(128)S(1)}, s32[128]{0:T(128)S(1)}, /*index=5*/bf16[256,2...) while((s32[]{:T(128)}, f32[128,2048]{0,1:T(8,128)S(1)}, ...), condition=%wide.region_35.36_spmd.clone, body=%wide.region_2.35_spmd.clone.sunk | while | flops 30148740 | bytes 21566524 | solution.py:79
  132.0 6.9 %bitcast_reduce_fusion.17 = (bf16[128,128]{0,1:T(8,128)(2,1)S(1)}, bf16[128,128]{0,1:T(8,128)(2,1)S(1)}, bf16[128,128]{0,1:T(8,128)(2,1)S(1)}, bf16[128,128]{0,1...) fusion(f32[128,2048]{0,1:T(8,128)S(1)} %get-tuple-element.1035,, ...), kind=kLoop, calls=%fused_computation.64.clone.1 | loop fusion | flops 12320768 | bytes 9961536 | tf_op jit(solution)/shard_map/while/body/eval_jaxpr/reduce_sum | solution.py:71
  143.3 9.6 %fusion.126 = f32[128,2048]{0,1:T(8,128)S(1)} fusion(f32[128,2048]{0,1:T(8,128)S(1)} %get-tuple-element.987, f32[2048]{0:T(1024)S(1)} %mul.1386, f32[2048]{0:T(1024)S(1)} %mul.1387, f32[2048]{0:T(1024)S(1)} %mul.1388, f32[2048]{0:T(1024)S(1)} %mul.1389, f32[2048]{0:T(1024)S(1)} %mul.1390, f32[2048]{0:T(1024)S(1)} %mul.1391, f32[2048]{0:T(1024)S(1)} %mul.1392, ...), kind=kLoop, calls=%fused_computation.48.clone.1 | loop fusion | flops 17039360 | bytes 10618945 | tf_op jit(solution)/shard_map/while/body/eval_jaxpr/add | solution.py:70
  154.3 6.9 %bitcast_reduce_fusion.17 = (bf16[128,128]{0,1:T(8,128)(2,1)S(1)}, bf16[128,128]{0,1:T(8,128)(2,1)S(1)}, bf16[128,128]{0,1:T(8,128)(2,1)S(1)}, bf16[128,128]{0,1...) fusion(f32[128,2048]{0,1:T(8,128)S(1)} %get-tuple-element.1035,, ...), kind=kLoop, calls=%fused_computation.64.clone.1 | loop fusion | flops 12320768 | bytes 9961536 | tf_op jit(solution)/shard_map/while/body/eval_jaxpr/reduce_sum | solution.py:71
  165.7 9.6 %fusion.126 = f32[128,2048]{0,1:T(8,128)S(1)} fusion(f32[128,2048]{0,1:T(8,128)S(1)} %get-tuple-element.987, f32[2048]{0:T(1024)S(1)} %mul.1386, f32[2048]{0:T(1024)S(1)} %mul.1387, f32[2048]{0:T(1024)S(1)} %mul.1388, f32[2048]{0:T(1024)S(1)} %mul.1389, f32[2048]{0:T(1024)S(1)} %mul.1390, f32[2048]{0:T(1024)S(1)} %mul.1391, f32[2048]{0:T(1024)S(1)} %mul.1392, ...), kind=kLoop, calls=%fused_computation.48.clone.1 | loop fusion | flops 17039360 | bytes 10618945 | tf_op jit(solution)/shard_map/while/body/eval_jaxpr/add | solution.py:70
  176.7 6.9 %bitcast_reduce_fusion.17 = (bf16[128,128]{0,1:T(8,128)(2,1)S(1)}, bf16[128,128]{0,1:T(8,128)(2,1)S(1)}, bf16[128,128]{0,1:T(8,128)(2,1)S(1)}, bf16[128,128]{0,1...) fusion(f32[128,2048]{0,1:T(8,128)S(1)} %get-tuple-element.1035,, ...), kind=kLoop, calls=%fused_computation.64.clone.1 | loop fusion | flops 12320768 | bytes 9961536 | tf_op jit(solution)/shard_map/while/body/eval_jaxpr/reduce_sum | solution.py:71
  188.0 9.6 %fusion.126 = f32[128,2048]{0,1:T(8,128)S(1)} fusion(f32[128,2048]{0,1:T(8,128)S(1)} %get-tuple-element.987, f32[2048]{0:T(1024)S(1)} %mul.1386, f32[2048]{0:T(1024)S(1)} %mul.1387, f32[2048]{0:T(1024)S(1)} %mul.1388, f32[2048]{0:T(1024)S(1)} %mul.1389, f32[2048]{0:T(1024)S(1)} %mul.1390, f32[2048]{0:T(1024)S(1)} %mul.1391, f32[2048]{0:T(1024)S(1)} %mul.1392, ...), kind=kLoop, calls=%fused_computation.48.clone.1 | loop fusion | flops 17039360 | bytes 10618945 | tf_op jit(solution)/shard_map/while/body/eval_jaxpr/add | solution.py:70
  199.0 6.9 %bitcast_reduce_fusion.17 = (bf16[128,128]{0,1:T(8,128)(2,1)S(1)}, bf16[128,128]{0,1:T(8,128)(2,1)S(1)}, bf16[128,128]{0,1:T(8,128)(2,1)S(1)}, bf16[128,128]{0,1...) fusion(f32[128,2048]{0,1:T(8,128)S(1)} %get-tuple-element.1035,, ...), kind=kLoop, calls=%fused_computation.64.clone.1 | loop fusion | flops 12320768 | bytes 9961536 | tf_op jit(solution)/shard_map/while/body/eval_jaxpr/reduce_sum | solution.py:71
  210.3 9.6 %fusion.126 = f32[128,2048]{0,1:T(8,128)S(1)} fusion(f32[128,2048]{0,1:T(8,128)S(1)} %get-tuple-element.987, f32[2048]{0:T(1024)S(1)} %mul.1386, f32[2048]{0:T(1024)S(1)} %mul.1387, f32[2048]{0:T(1024)S(1)} %mul.1388, f32[2048]{0:T(1024)S(1)} %mul.1389, f32[2048]{0:T(1024)S(1)} %mul.1390, f32[2048]{0:T(1024)S(1)} %mul.1391, f32[2048]{0:T(1024)S(1)} %mul.1392, ...), kind=kLoop, calls=%fused_computation.48.clone.1 | loop fusion | flops 17039360 | bytes 10618945 | tf_op jit(solution)/shard_map/while/body/eval_jaxpr/add | solution.py:70
  221.3 6.9 %bitcast_reduce_fusion.17 = (bf16[128,128]{0,1:T(8,128)(2,1)S(1)}, bf16[128,128]{0,1:T(8,128)(2,1)S(1)}, bf16[128,128]{0,1:T(8,128)(2,1)S(1)}, bf16[128,128]{0,1...) fusion(f32[128,2048]{0,1:T(8,128)S(1)} %get-tuple-element.1035,, ...), kind=kLoop, calls=%fused_computation.64.clone.1 | loop fusion | flops 12320768 | bytes 9961536 | tf_op jit(solution)/shard_map/while/body/eval_jaxpr/reduce_sum | solution.py:71
  232.7 9.6 %fusion.126 = f32[128,2048]{0,1:T(8,128)S(1)} fusion(f32[128,2048]{0,1:T(8,128)S(1)} %get-tuple-element.987, f32[2048]{0:T(1024)S(1)} %mul.1386, f32[2048]{0:T(1024)S(1)} %mul.1387, f32[2048]{0:T(1024)S(1)} %mul.1388, f32[2048]{0:T(1024)S(1)} %mul.1389, f32[2048]{0:T(1024)S(1)} %mul.1390, f32[2048]{0:T(1024)S(1)} %mul.1391, f32[2048]{0:T(1024)S(1)} %mul.1392, ...), kind=kLoop, calls=%fused_computation.48.clone.1 | loop fusion | flops 17039360 | bytes 10618945 | tf_op jit(solution)/shard_map/while/body/eval_jaxpr/add | solution.py:70
  243.6 6.9 %bitcast_reduce_fusion.17 = (bf16[128,128]{0,1:T(8,128)(2,1)S(1)}, bf16[128,128]{0,1:T(8,128)(2,1)S(1)}, bf16[128,128]{0,1:T(8,128)(2,1)S(1)}, bf16[128,128]{0,1...) fusion(f32[128,2048]{0,1:T(8,128)S(1)} %get-tuple-element.1035,, ...), kind=kLoop, calls=%fused_computation.64.clone.1 | loop fusion | flops 12320768 | bytes 9961536 | tf_op jit(solution)/shard_map/while/body/eval_jaxpr/reduce_sum | solution.py:71
  255.0 9.6 %fusion.126 = f32[128,2048]{0,1:T(8,128)S(1)} fusion(f32[128,2048]{0,1:T(8,128)S(1)} %get-tuple-element.987, f32[2048]{0:T(1024)S(1)} %mul.1386, f32[2048]{0:T(1024)S(1)} %mul.1387, f32[2048]{0:T(1024)S(1)} %mul.1388, f32[2048]{0:T(1024)S(1)} %mul.1389, f32[2048]{0:T(1024)S(1)} %mul.1390, f32[2048]{0:T(1024)S(1)} %mul.1391, f32[2048]{0:T(1024)S(1)} %mul.1392, ...), kind=kLoop, calls=%fused_computation.48.clone.1 | loop fusion | flops 17039360 | bytes 10618945 | tf_op jit(solution)/shard_map/while/body/eval_jaxpr/add | solution.py:70
  266.0 6.9 %bitcast_reduce_fusion.17 = (bf16[128,128]{0,1:T(8,128)(2,1)S(1)}, bf16[128,128]{0,1:T(8,128)(2,1)S(1)}, bf16[128,128]{0,1:T(8,128)(2,1)S(1)}, bf16[128,128]{0,1...) fusion(f32[128,2048]{0,1:T(8,128)S(1)} %get-tuple-element.1035,, ...), kind=kLoop, calls=%fused_computation.64.clone.1 | loop fusion | flops 12320768 | bytes 9961536 | tf_op jit(solution)/shard_map/while/body/eval_jaxpr/reduce_sum | solution.py:71
  277.3 9.6 %fusion.126 = f32[128,2048]{0,1:T(8,128)S(1)} fusion(f32[128,2048]{0,1:T(8,128)S(1)} %get-tuple-element.987, f32[2048]{0:T(1024)S(1)} %mul.1386, f32[2048]{0:T(1024)S(1)} %mul.1387, f32[2048]{0:T(1024)S(1)} %mul.1388, f32[2048]{0:T(1024)S(1)} %mul.1389, f32[2048]{0:T(1024)S(1)} %mul.1390, f32[2048]{0:T(1024)S(1)} %mul.1391, f32[2048]{0:T(1024)S(1)} %mul.1392, ...), kind=kLoop, calls=%fused_computation.48.clone.1 | loop fusion | flops 17039360 | bytes 10618945 | tf_op jit(solution)/shard_map/while/body/eval_jaxpr/add | solution.py:70
  288.3 6.9 %bitcast_reduce_fusion.17 = (bf16[128,128]{0,1:T(8,128)(2,1)S(1)}, bf16[128,128]{0,1:T(8,128)(2,1)S(1)}, bf16[128,128]{0,1:T(8,128)(2,1)S(1)}, bf16[128,128]{0,1...) fusion(f32[128,2048]{0,1:T(8,128)S(1)} %get-tuple-element.1035,, ...), kind=kLoop, calls=%fused_computation.64.clone.1 | loop fusion | flops 12320768 | bytes 9961536 | tf_op jit(solution)/shard_map/while/body/eval_jaxpr/reduce_sum | solution.py:71
  299.6 9.6 %fusion.126 = f32[128,2048]{0,1:T(8,128)S(1)} fusion(f32[128,2048]{0,1:T(8,128)S(1)} %get-tuple-element.987, f32[2048]{0:T(1024)S(1)} %mul.1386, f32[2048]{0:T(1024)S(1)} %mul.1387, f32[2048]{0:T(1024)S(1)} %mul.1388, f32[2048]{0:T(1024)S(1)} %mul.1389, f32[2048]{0:T(1024)S(1)} %mul.1390, f32[2048]{0:T(1024)S(1)} %mul.1391, f32[2048]{0:T(1024)S(1)} %mul.1392, ...), kind=kLoop, calls=%fused_computation.48.clone.1 | loop fusion | flops 17039360 | bytes 10618945 | tf_op jit(solution)/shard_map/while/body/eval_jaxpr/add | solution.py:70
  314.6 2.6 fusion.111
  317.2 85.1 %all-reduce.2.cloned.1.call-done = f32[128,128]{1,0:T(8,128)} async-done(((f32[128,128]{1,0:T(8,128)}), f32[128,128]{1,0:T(8,128)}) %all-reduce.2.cloned.1.call-update) | async-done | bytes 65552 | tf_op jit(solution)/shard_map/psum | solution.py:103
  (697 shorter events, 88.6 us)
Async XLA Ops:
  7.2 395.1 %all-reduce.2.cloned.1.call-start = ((), (), s32[]{:S(2)}) async-start(), calls=%async_computation | async-start | bytes 131072 | tf_op jit(solution)/shard_map/psum | solution.py:103
  7.2 24.1 %copy-start.5 = (bf16[1,128,128]{2,1,0:T(8,128)(2,1)S(1)}, bf16[1,128,128]{2,1,0:T(8,128)(2,1)}, u32[]{:S(2)}) copy-start(bf16[1,128,128]{2,1,0:T(8,128)(2,1)} %param.11) | copy-start | bytes 98308
  7.2 13.9 %collective-permute-start = (bf16[128,2048]{1,0:T(8,128)(2,1)}, bf16[128,2048]{1,0:T(8,128)(2,1)S(1)}, u32[]{:S(2)}, u32[]{:S(2)}) collective-permute-start(bf16[128,2048]{1,0:T(8,128)(2,1)} %bitcast.309), channel_id=1, source_target_pairs={{0,16},{16,0},{1,17},{17,1},{2,18},{18,2},{3,19},{19,3},{4,20},{20... | collective-permute-start | bytes 1572872 | tf_op jit(solution)/shard_map/ppermute | solution.py:10
  21.2 3.4 copy-start.4
  22.6 8.7 %copy-start.2 = (bf16[128,2048]{1,0:T(8,128)(2,1)}, bf16[128,2048]{1,0:T(8,128)(2,1)S(1)}, u32[]{:S(2)}) copy-start(bf16[128,2048]{1,0:T(8,128)(2,1)S(1)} %fusion.112) | copy-start | bytes 1572868
  22.6 8.6 %collective-permute-start.2 = (bf16[128,2048]{1,0:T(8,128)(2,1)S(1)}, bf16[128,2048]{1,0:T(8,128)(2,1)S(1)}, u32[]{:S(2)}, u32[]{:S(2)}) collective-permute-start(bf16[128,2048]{1,0:T(8,128)(2,1)S(1)} %fusion.112), channel_id=1, source_target_pairs={{1,0},{2,1},{3,2},{4,3},{5,4},{6,5},{7,6},{8,7},{9,8},{10,9},{11,1... | collective-permute-start | bytes 1572872 | tf_op jit(solution)/shard_map/ppermute | solution.py:16
  112.7 6.4 %copy-start.6 = (bf16[1,3,3,2048]{3,2,1,0:T(4,128)(2,1)S(1)}, bf16[1,3,3,2048]{3,2,1,0:T(4,128)(2,1)}, u32[]{:S(2)}) copy-start(bf16[1,3,3,2048]{3,2,1,0:T(4,128)(2,1)} %param.12) | copy-start | bytes 110596
  112.7 6.6 %copy-start.3 = (bf16[128,2048]{1,0:T(8,128)(2,1)S(1)}, bf16[128,2048]{1,0:T(8,128)(2,1)}, u32[]{:S(2)}) copy-start(bf16[128,2048]{1,0:T(8,128)(2,1)} %copy-done.2) | copy-start | bytes 1572868
  115.3 11.7 %collective-permute-start.1 = (bf16[128,2048]{1,0:T(8,128)(2,1)S(1)}, bf16[128,2048]{1,0:T(8,128)(2,1)}, u32[]{:S(2)}, u32[]{:S(2)}) collective-permute-start(bf16[128,2048]{1,0:T(8,128)(2,1)S(1)} %get-tuple-element.492), channel_id=1, source_target_pairs={{0,1},{1,2},{2,3},{3,4},{4,5},{5,6},{6,7},{7,8},{8,9},{9,10},{10,1... | collective-permute-start | bytes 1572872 | tf_op jit(solution)/shard_map/ppermute | solution.py:16
  309.2 1.5 copy-start
  309.2 1.5 copy-start.1
  311.0 3.4 collective-permute-start.3
Sparse Core Ops, SparseCore 0:
  313.2 89.0 all-reduce.1
where the time goes:
time: 411 us
  other arithmetic  200 us (49%)
  waiting for transfers between devices  111 us (27%)
  local copies, waits for them, and re-layouts  61.2 us (15%)
  between operations  14.3 us (3%)
  loops' own time  14.2 us (3%)
  starting transfers between devices  9.31 us (2%)
    psum x1, waiting for transfers between devices, body(): summed = lax.psum(filter_sum, 'ctx')  85.1 us
    add x8, other arithmetic, forward_step(): total = total + jnp.where(usable, shifted * weights[None, :], 0.0)  76.8 us
    reduce_sum x8, other arithmetic, forward_step(): jnp.sum((grad_wide * shifted).reshape(row_count, groups, members), axis=2)  55.5 us
    add x8, other arithmetic, step(): total + jnp.where((lag <= ahead_pos)[:, None], ahead * weights[None, :],...  44.8 us
    ppermute x3, waiting for transfers between devices, shifted_2(): return lax.ppermute(block, axis, route)  13.8 us
    ppermute x1, waiting for transfers between devices, from_behind(): lax.ppermute(shard, axis, [(i, (i + by) % count) for i in range(count)])  12.4 us
    mul x128, local copies, waits for them, and re-layouts, step(): ahead * weights[None, :]  12.2 us
    mul x128, local copies, waits for them, and re-layouts, forward_step(): total = total + jnp.where(usable, shifted * weights[None, :], 0.0)  12.2 us
  transfers between devices with their start and end apart: 5, of which 5 were waited for; matrix products, arithmetic and copies ran while one was open for 1% of the time, Pallas kernels for 0%

commit v1 on v0

--- a/solution.py
+++ b/solution.py
@@ -100,7 +100,9 @@
             0.0,
         )
     grad_pre = total.astype(jnp.bfloat16)[None]
-    summed = lax.psum(filter_sum, "ctx")
+    summed = filter_sum
+    for hop in (1, 2, 4, 8):
+        summed = summed + lax.ppermute(summed, "ctx", [(dev, dev ^ hop) for dev in range(16)])
     filter_grad = (summed / math.sqrt(row_count * devices * members))[None]
     return (grad_pre, filter_grad)
 

time: 411 us -> 324 us (0.79)
  waiting for transfers between devices: 111 us -> 31.5 us
  between operations: 14.3 us -> 0.95 us
  starting transfers between devices: 9.31 us -> 14.2 us
    psum x1 -> x0, waiting for transfers between devices: 85.1 us -> none  [body(): summed = lax.psum(filter_sum, 'ctx')]
    ppermute x0 -> x4, waiting for transfers between devices: none -> 6.72 us  [body(): lax.ppermute(summed, 'ctx', [(dev, dev ^ hop) for dev in range(16)])]
    ppermute x0 -> x4, starting transfers between devices: none -> 4.34 us  [body(): lax.ppermute(summed, 'ctx', [(dev, dev ^ hop) for dev in range(16)])]
  transfers between devices with their start and end apart: 5 -> 8, of which waited for: 5 -> 5; matrix products, arithmetic and copies ran while one was open for 1% -> 2% of each run, Pallas kernels for 0% -> 0%
where the time goes in v1:
time: 324 us; the launch traced here: 322 us
  other arithmetic  200 us (62%)
  local copies, waits for them, and re-layouts  61.2 us (19%)
  waiting for transfers between devices  31.5 us (10%)
  loops' own time  14.3 us (4%)
  starting transfers between devices  14.2 us (4%)
    add x8, other arithmetic, forward_step(): total = total + jnp.where(usable, shifted * weights[None, :], 0.0)  76.4 us
    reduce_sum x8, other arithmetic, forward_step(): jnp.sum((grad_wide * shifted).reshape(row_count, groups, members), axis=2)  55 us
    add x8, other arithmetic, step(): total + jnp.where((lag <= ahead_pos)[:, None], ahead * weights[None, :],...  44.8 us
    ppermute x3, waiting for transfers between devices, shifted_2(): return lax.ppermute(block, axis, route)  12.5 us
    ppermute x1, waiting for transfers between devices, from_behind(): lax.ppermute(shard, axis, [(i, (i + by) % count) for i in range(count)])  12.4 us
    mul x128, local copies, waits for them, and re-layouts, step(): ahead * weights[None, :]  12.2 us
    mul x128, local copies, waits for them, and re-layouts, forward_step(): total = total + jnp.where(usable, shifted * weights[None, :], 0.0)  12.2 us
    dynamic_slice x16, local copies, waits for them, and re-layouts, body(): lax.scan(forward_step, jnp.zeros((row_count, channels), jnp.float32), bases)  10 us
  transfers between devices with their start and end apart: 8, of which 5 were waited for; matrix products, arithmetic and copies ran while one was open for 2% of the time, Pallas kernels for 0%

profile of v1, /device:TPU:8, one launch (start us, length us, event | category | flops | bytes accessed | tf_op | source)
XLA Modules:
  0.0 321.6 jit_solution(1417006654464104880)
XLA Ops:
  2.2 12.4 %collective-permute-done = bf16[128,2048]{1,0:T(8,128)(2,1)S(1)} collective-permute-done((bf16[128,2048]{1,0:T(8,128)(2,1)}, bf16[128,2048]{1,0:T(8,128)(2,1)S(1)}, u32[]{:S(2)}, u32[]{:S(2)}) %collective-permute-start) | collective-permute-done | bytes 524320 | tf_op jit(solution)/shard_map/ppermute | solution.py:10
  19.6 5.0 %collective-permute-done.2 = bf16[128,2048]{1,0:T(8,128)(2,1)S(1)} collective-permute-done((bf16[128,2048]{1,0:T(8,128)(2,1)S(1)}, bf16[128,2048]{1,0:T(8,128)(2,1)S(1)}, u32[]{:S(2)}, u32[]{:S(2)}) %collective-permute-start.2) | collective-permute-done | bytes 524320 | tf_op jit(solution)/shard_map/ppermute | solution.py:16
  24.8 81.4 %while.30 = (s32[]{:T(128)}, f32[128,2048]{1,0:T(8,128)S(1)}, s32[8]{0:T(128)S(1)}, s32[256]{0:T(256)S(1)}, bf16[256,2048]{1,0:T(8,128)(2,1)S(1)}, /*index=5*/bf...) while((s32[]{:T(128)}, f32[128,2048]{1,0:T(8,128)S(1)}, ...), condition=%wide.region_37.38_spmd.clone, body=%wide.region_36.37_spmd.clone.sunk | while | flops 17043556 | bytes 11044691 | solution.py:33
  29.3 5.6 %fusion.128 = f32[128,2048]{1,0:T(8,128)S(1)} fusion(f32[128,2048]{1,0:T(8,128)S(1)} %get-tuple-element.835, f32[2048]{0:T(1024)S(1)} %mul.1435, bf16[256,2048]{1,0:T(8,128)(2,1)S(1)} %get-tuple-element.893, s32[]{:T(128)S(6)} %select_n.1196, f32[2048]{0:T(1024)S(1)} %mul.1436, s32[]{:T(128)S(6)} %select_n.1197, f32[2048]{0:T(1024)S(1)} %mul.1437, ...), kind=kLoop, calls=%fused_computation.176.clone.1 | loop fusion | flops 17039360 | bytes 10618945 | tf_op jit(solution)/shard_map/while/body/eval_jaxpr/add | solution.py:29
  39.5 5.6 %fusion.128 = f32[128,2048]{1,0:T(8,128)S(1)} fusion(f32[128,2048]{1,0:T(8,128)S(1)} %get-tuple-element.835, f32[2048]{0:T(1024)S(1)} %mul.1435, bf16[256,2048]{1,0:T(8,128)(2,1)S(1)} %get-tuple-element.893, s32[]{:T(128)S(6)} %select_n.1196, f32[2048]{0:T(1024)S(1)} %mul.1436, s32[]{:T(128)S(6)} %select_n.1197, f32[2048]{0:T(1024)S(1)} %mul.1437, ...), kind=kLoop, calls=%fused_computation.176.clone.1 | loop fusion | flops 17039360 | bytes 10618945 | tf_op jit(solution)/shard_map/while/body/eval_jaxpr/add | solution.py:29
  49.7 5.6 %fusion.128 = f32[128,2048]{1,0:T(8,128)S(1)} fusion(f32[128,2048]{1,0:T(8,128)S(1)} %get-tuple-element.835, f32[2048]{0:T(1024)S(1)} %mul.1435, bf16[256,2048]{1,0:T(8,128)(2,1)S(1)} %get-tuple-element.893, s32[]{:T(128)S(6)} %select_n.1196, f32[2048]{0:T(1024)S(1)} %mul.1436, s32[]{:T(128)S(6)} %select_n.1197, f32[2048]{0:T(1024)S(1)} %mul.1437, ...), kind=kLoop, calls=%fused_computation.176.clone.1 | loop fusion | flops 17039360 | bytes 10618945 | tf_op jit(solution)/shard_map/while/body/eval_jaxpr/add | solution.py:29
  59.8 5.6 %fusion.128 = f32[128,2048]{1,0:T(8,128)S(1)} fusion(f32[128,2048]{1,0:T(8,128)S(1)} %get-tuple-element.835, f32[2048]{0:T(1024)S(1)} %mul.1435, bf16[256,2048]{1,0:T(8,128)(2,1)S(1)} %get-tuple-element.893, s32[]{:T(128)S(6)} %select_n.1196, f32[2048]{0:T(1024)S(1)} %mul.1436, s32[]{:T(128)S(6)} %select_n.1197, f32[2048]{0:T(1024)S(1)} %mul.1437, ...), kind=kLoop, calls=%fused_computation.176.clone.1 | loop fusion | flops 17039360 | bytes 10618945 | tf_op jit(solution)/shard_map/while/body/eval_jaxpr/add | solution.py:29
  70.0 5.6 %fusion.128 = f32[128,2048]{1,0:T(8,128)S(1)} fusion(f32[128,2048]{1,0:T(8,128)S(1)} %get-tuple-element.835, f32[2048]{0:T(1024)S(1)} %mul.1435, bf16[256,2048]{1,0:T(8,128)(2,1)S(1)} %get-tuple-element.893, s32[]{:T(128)S(6)} %select_n.1196, f32[2048]{0:T(1024)S(1)} %mul.1436, s32[]{:T(128)S(6)} %select_n.1197, f32[2048]{0:T(1024)S(1)} %mul.1437, ...), kind=kLoop, calls=%fused_computation.176.clone.1 | loop fusion | flops 17039360 | bytes 10618945 | tf_op jit(solution)/shard_map/while/body/eval_jaxpr/add | solution.py:29
  80.2 5.6 %fusion.128 = f32[128,2048]{1,0:T(8,128)S(1)} fusion(f32[128,2048]{1,0:T(8,128)S(1)} %get-tuple-element.835, f32[2048]{0:T(1024)S(1)} %mul.1435, bf16[256,2048]{1,0:T(8,128)(2,1)S(1)} %get-tuple-element.893, s32[]{:T(128)S(6)} %select_n.1196, f32[2048]{0:T(1024)S(1)} %mul.1436, s32[]{:T(128)S(6)} %select_n.1197, f32[2048]{0:T(1024)S(1)} %mul.1437, ...), kind=kLoop, calls=%fused_computation.176.clone.1 | loop fusion | flops 17039360 | bytes 10618945 | tf_op jit(solution)/shard_map/while/body/eval_jaxpr/add | solution.py:29
  90.3 5.6 %fusion.128 = f32[128,2048]{1,0:T(8,128)S(1)} fusion(f32[128,2048]{1,0:T(8,128)S(1)} %get-tuple-element.835, f32[2048]{0:T(1024)S(1)} %mul.1435, bf16[256,2048]{1,0:T(8,128)(2,1)S(1)} %get-tuple-element.893, s32[]{:T(128)S(6)} %select_n.1196, f32[2048]{0:T(1024)S(1)} %mul.1436, s32[]{:T(128)S(6)} %select_n.1197, f32[2048]{0:T(1024)S(1)} %mul.1437, ...), kind=kLoop, calls=%fused_computation.176.clone.1 | loop fusion | flops 17039360 | bytes 10618945 | tf_op jit(solution)/shard_map/while/body/eval_jaxpr/add | solution.py:29
  100.5 5.6 %fusion.128 = f32[128,2048]{1,0:T(8,128)S(1)} fusion(f32[128,2048]{1,0:T(8,128)S(1)} %get-tuple-element.835, f32[2048]{0:T(1024)S(1)} %mul.1435, bf16[256,2048]{1,0:T(8,128)(2,1)S(1)} %get-tuple-element.893, s32[]{:T(128)S(6)} %select_n.1196, f32[2048]{0:T(1024)S(1)} %mul.1436, s32[]{:T(128)S(6)} %select_n.1197, f32[2048]{0:T(1024)S(1)} %mul.1437, ...), kind=kLoop, calls=%fused_computation.176.clone.1 | loop fusion | flops 17039360 | bytes 10618945 | tf_op jit(solution)/shard_map/while/body/eval_jaxpr/add | solution.py:29
  108.8 3.8 %collective-permute-start.1 = (bf16[128,2048]{1,0:T(8,128)(2,1)S(1)}, bf16[128,2048]{1,0:T(8,128)(2,1)}, u32[]{:S(2)}, u32[]{:S(2)}) collective-permute-start(bf16[128,2048]{1,0:T(8,128)(2,1)S(1)} %get-tuple-element.492), channel_id=1, source_target_pairs={{0,1},{1,2},{2,3},{3,4},{4,5},{5,6},{6,7},{7,8},{8,9},{9,10},{10,1... | collective-permute-start | bytes 1572872 | tf_op jit(solution)/shard_map/ppermute | solution.py:16
  113.0 7.5 %collective-permute-done.1 = bf16[128,2048]{1,0:T(8,128)(2,1)} collective-permute-done((bf16[128,2048]{1,0:T(8,128)(2,1)S(1)}, bf16[128,2048]{1,0:T(8,128)(2,1)}, u32[]{:S(2)}, u32[]{:S(2)}) %collective-permute-start.1) | collective-permute-done | bytes 524320 | tf_op jit(solution)/shard_map/ppermute | solution.py:16
  124.1 177.8 %while.29 = (s32[]{:T(128)}, f32[128,2048]{0,1:T(8,128)S(1)}, f32[8,16,128]{2,1,0:T(8,128)}, s32[8]{0:T(128)S(1)}, s32[128]{0:T(128)S(1)}, /*index=5*/bf16[256,2...) while((s32[]{:T(128)}, f32[128,2048]{0,1:T(8,128)S(1)}, ...), condition=%wide.region_35.36_spmd.clone, body=%wide.region_2.35_spmd.clone.sunk | while | flops 30148740 | bytes 21566524 | solution.py:79
  125.5 6.9 %bitcast_reduce_fusion.17 = (bf16[128,128]{0,1:T(8,128)(2,1)S(1)}, bf16[128,128]{0,1:T(8,128)(2,1)S(1)}, bf16[128,128]{0,1:T(8,128)(2,1)S(1)}, bf16[128,128]{0,1...) fusion(f32[128,2048]{0,1:T(8,128)S(1)} %get-tuple-element.1035,, ...), kind=kLoop, calls=%fused_computation.64.clone.1 | loop fusion | flops 12320768 | bytes 9961536 | tf_op jit(solution)/shard_map/while/body/eval_jaxpr/reduce_sum | solution.py:71
  136.8 9.6 %fusion.126 = f32[128,2048]{0,1:T(8,128)S(1)} fusion(f32[128,2048]{0,1:T(8,128)S(1)} %get-tuple-element.987, f32[2048]{0:T(1024)S(1)} %mul.1386, f32[2048]{0:T(1024)S(1)} %mul.1387, f32[2048]{0:T(1024)S(1)} %mul.1388, f32[2048]{0:T(1024)S(1)} %mul.1389, f32[2048]{0:T(1024)S(1)} %mul.1390, f32[2048]{0:T(1024)S(1)} %mul.1391, f32[2048]{0:T(1024)S(1)} %mul.1392, ...), kind=kLoop, calls=%fused_computation.48.clone.1 | loop fusion | flops 17039360 | bytes 10618945 | tf_op jit(solution)/shard_map/while/body/eval_jaxpr/add | solution.py:70
  147.7 6.9 %bitcast_reduce_fusion.17 = (bf16[128,128]{0,1:T(8,128)(2,1)S(1)}, bf16[128,128]{0,1:T(8,128)(2,1)S(1)}, bf16[128,128]{0,1:T(8,128)(2,1)S(1)}, bf16[128,128]{0,1...) fusion(f32[128,2048]{0,1:T(8,128)S(1)} %get-tuple-element.1035,, ...), kind=kLoop, calls=%fused_computation.64.clone.1 | loop fusion | flops 12320768 | bytes 9961536 | tf_op jit(solution)/shard_map/while/body/eval_jaxpr/reduce_sum | solution.py:71
  159.0 9.6 %fusion.126 = f32[128,2048]{0,1:T(8,128)S(1)} fusion(f32[128,2048]{0,1:T(8,128)S(1)} %get-tuple-element.987, f32[2048]{0:T(1024)S(1)} %mul.1386, f32[2048]{0:T(1024)S(1)} %mul.1387, f32[2048]{0:T(1024)S(1)} %mul.1388, f32[2048]{0:T(1024)S(1)} %mul.1389, f32[2048]{0:T(1024)S(1)} %mul.1390, f32[2048]{0:T(1024)S(1)} %mul.1391, f32[2048]{0:T(1024)S(1)} %mul.1392, ...), kind=kLoop, calls=%fused_computation.48.clone.1 | loop fusion | flops 17039360 | bytes 10618945 | tf_op jit(solution)/shard_map/while/body/eval_jaxpr/add | solution.py:70
  170.0 6.9 %bitcast_reduce_fusion.17 = (bf16[128,128]{0,1:T(8,128)(2,1)S(1)}, bf16[128,128]{0,1:T(8,128)(2,1)S(1)}, bf16[128,128]{0,1:T(8,128)(2,1)S(1)}, bf16[128,128]{0,1...) fusion(f32[128,2048]{0,1:T(8,128)S(1)} %get-tuple-element.1035,, ...), kind=kLoop, calls=%fused_computation.64.clone.1 | loop fusion | flops 12320768 | bytes 9961536 | tf_op jit(solution)/shard_map/while/body/eval_jaxpr/reduce_sum | solution.py:71
  181.2 9.6 %fusion.126 = f32[128,2048]{0,1:T(8,128)S(1)} fusion(f32[128,2048]{0,1:T(8,128)S(1)} %get-tuple-element.987, f32[2048]{0:T(1024)S(1)} %mul.1386, f32[2048]{0:T(1024)S(1)} %mul.1387, f32[2048]{0:T(1024)S(1)} %mul.1388, f32[2048]{0:T(1024)S(1)} %mul.1389, f32[2048]{0:T(1024)S(1)} %mul.1390, f32[2048]{0:T(1024)S(1)} %mul.1391, f32[2048]{0:T(1024)S(1)} %mul.1392, ...), kind=kLoop, calls=%fused_computation.48.clone.1 | loop fusion | flops 17039360 | bytes 10618945 | tf_op jit(solution)/shard_map/while/body/eval_jaxpr/add | solution.py:70
  192.2 6.9 %bitcast_reduce_fusion.17 = (bf16[128,128]{0,1:T(8,128)(2,1)S(1)}, bf16[128,128]{0,1:T(8,128)(2,1)S(1)}, bf16[128,128]{0,1:T(8,128)(2,1)S(1)}, bf16[128,128]{0,1...) fusion(f32[128,2048]{0,1:T(8,128)S(1)} %get-tuple-element.1035,, ...), kind=kLoop, calls=%fused_computation.64.clone.1 | loop fusion | flops 12320768 | bytes 9961536 | tf_op jit(solution)/shard_map/while/body/eval_jaxpr/reduce_sum | solution.py:71
  203.5 9.6 %fusion.126 = f32[128,2048]{0,1:T(8,128)S(1)} fusion(f32[128,2048]{0,1:T(8,128)S(1)} %get-tuple-element.987, f32[2048]{0:T(1024)S(1)} %mul.1386, f32[2048]{0:T(1024)S(1)} %mul.1387, f32[2048]{0:T(1024)S(1)} %mul.1388, f32[2048]{0:T(1024)S(1)} %mul.1389, f32[2048]{0:T(1024)S(1)} %mul.1390, f32[2048]{0:T(1024)S(1)} %mul.1391, f32[2048]{0:T(1024)S(1)} %mul.1392, ...), kind=kLoop, calls=%fused_computation.48.clone.1 | loop fusion | flops 17039360 | bytes 10618945 | tf_op jit(solution)/shard_map/while/body/eval_jaxpr/add | solution.py:70
  214.4 6.9 %bitcast_reduce_fusion.17 = (bf16[128,128]{0,1:T(8,128)(2,1)S(1)}, bf16[128,128]{0,1:T(8,128)(2,1)S(1)}, bf16[128,128]{0,1:T(8,128)(2,1)S(1)}, bf16[128,128]{0,1...) fusion(f32[128,2048]{0,1:T(8,128)S(1)} %get-tuple-element.1035,, ...), kind=kLoop, calls=%fused_computation.64.clone.1 | loop fusion | flops 12320768 | bytes 9961536 | tf_op jit(solution)/shard_map/while/body/eval_jaxpr/reduce_sum | solution.py:71
  225.7 9.6 %fusion.126 = f32[128,2048]{0,1:T(8,128)S(1)} fusion(f32[128,2048]{0,1:T(8,128)S(1)} %get-tuple-element.987, f32[2048]{0:T(1024)S(1)} %mul.1386, f32[2048]{0:T(1024)S(1)} %mul.1387, f32[2048]{0:T(1024)S(1)} %mul.1388, f32[2048]{0:T(1024)S(1)} %mul.1389, f32[2048]{0:T(1024)S(1)} %mul.1390, f32[2048]{0:T(1024)S(1)} %mul.1391, f32[2048]{0:T(1024)S(1)} %mul.1392, ...), kind=kLoop, calls=%fused_computation.48.clone.1 | loop fusion | flops 17039360 | bytes 10618945 | tf_op jit(solution)/shard_map/while/body/eval_jaxpr/add | solution.py:70
  236.6 6.9 %bitcast_reduce_fusion.17 = (bf16[128,128]{0,1:T(8,128)(2,1)S(1)}, bf16[128,128]{0,1:T(8,128)(2,1)S(1)}, bf16[128,128]{0,1:T(8,128)(2,1)S(1)}, bf16[128,128]{0,1...) fusion(f32[128,2048]{0,1:T(8,128)S(1)} %get-tuple-element.1035,, ...), kind=kLoop, calls=%fused_computation.64.clone.1 | loop fusion | flops 12320768 | bytes 9961536 | tf_op jit(solution)/shard_map/while/body/eval_jaxpr/reduce_sum | solution.py:71
  247.9 9.6 %fusion.126 = f32[128,2048]{0,1:T(8,128)S(1)} fusion(f32[128,2048]{0,1:T(8,128)S(1)} %get-tuple-element.987, f32[2048]{0:T(1024)S(1)} %mul.1386, f32[2048]{0:T(1024)S(1)} %mul.1387, f32[2048]{0:T(1024)S(1)} %mul.1388, f32[2048]{0:T(1024)S(1)} %mul.1389, f32[2048]{0:T(1024)S(1)} %mul.1390, f32[2048]{0:T(1024)S(1)} %mul.1391, f32[2048]{0:T(1024)S(1)} %mul.1392, ...), kind=kLoop, calls=%fused_computation.48.clone.1 | loop fusion | flops 17039360 | bytes 10618945 | tf_op jit(solution)/shard_map/while/body/eval_jaxpr/add | solution.py:70
  258.9 6.9 %bitcast_reduce_fusion.17 = (bf16[128,128]{0,1:T(8,128)(2,1)S(1)}, bf16[128,128]{0,1:T(8,128)(2,1)S(1)}, bf16[128,128]{0,1:T(8,128)(2,1)S(1)}, bf16[128,128]{0,1...) fusion(f32[128,2048]{0,1:T(8,128)S(1)} %get-tuple-element.1035,, ...), kind=kLoop, calls=%fused_computation.64.clone.1 | loop fusion | flops 12320768 | bytes 9961536 | tf_op jit(solution)/shard_map/while/body/eval_jaxpr/reduce_sum | solution.py:71
  270.1 9.6 %fusion.126 = f32[128,2048]{0,1:T(8,128)S(1)} fusion(f32[128,2048]{0,1:T(8,128)S(1)} %get-tuple-element.987, f32[2048]{0:T(1024)S(1)} %mul.1386, f32[2048]{0:T(1024)S(1)} %mul.1387, f32[2048]{0:T(1024)S(1)} %mul.1388, f32[2048]{0:T(1024)S(1)} %mul.1389, f32[2048]{0:T(1024)S(1)} %mul.1390, f32[2048]{0:T(1024)S(1)} %mul.1391, f32[2048]{0:T(1024)S(1)} %mul.1392, ...), kind=kLoop, calls=%fused_computation.48.clone.1 | loop fusion | flops 17039360 | bytes 10618945 | tf_op jit(solution)/shard_map/while/body/eval_jaxpr/add | solution.py:70
  281.1 6.9 %bitcast_reduce_fusion.17 = (bf16[128,128]{0,1:T(8,128)(2,1)S(1)}, bf16[128,128]{0,1:T(8,128)(2,1)S(1)}, bf16[128,128]{0,1:T(8,128)(2,1)S(1)}, bf16[128,128]{0,1...) fusion(f32[128,2048]{0,1:T(8,128)S(1)} %get-tuple-element.1035,, ...), kind=kLoop, calls=%fused_computation.64.clone.1 | loop fusion | flops 12320768 | bytes 9961536 | tf_op jit(solution)/shard_map/while/body/eval_jaxpr/reduce_sum | solution.py:71
  292.4 9.6 %fusion.126 = f32[128,2048]{0,1:T(8,128)S(1)} fusion(f32[128,2048]{0,1:T(8,128)S(1)} %get-tuple-element.987, f32[2048]{0:T(1024)S(1)} %mul.1386, f32[2048]{0:T(1024)S(1)} %mul.1387, f32[2048]{0:T(1024)S(1)} %mul.1388, f32[2048]{0:T(1024)S(1)} %mul.1389, f32[2048]{0:T(1024)S(1)} %mul.1390, f32[2048]{0:T(1024)S(1)} %mul.1391, f32[2048]{0:T(1024)S(1)} %mul.1392, ...), kind=kLoop, calls=%fused_computation.48.clone.1 | loop fusion | flops 17039360 | bytes 10618945 | tf_op jit(solution)/shard_map/while/body/eval_jaxpr/add | solution.py:70
  311.6 4.1 %collective-permute-done.6 = f32[128,128]{1,0:T(8,128)S(1)} collective-permute-done((f32[128,128]{1,0:T(8,128)S(1)}, f32[128,128]{1,0:T(8,128)S(1)}, u32[]{:S(2)}, u32[]{:S(2)}) %collective-permute-start.6) | collective-permute-done | bytes 65568 | tf_op jit(solution)/shard_map/ppermute | solution.py:105
  315.7 2.7 collective-permute-start.7
  (705 shorter events, 94.7 us)
Async XLA Ops:
  0.6 24.1 %copy-start.5 = (bf16[1,128,128]{2,1,0:T(8,128)(2,1)S(1)}, bf16[1,128,128]{2,1,0:T(8,128)(2,1)}, u32[]{:S(2)}) copy-start(bf16[1,128,128]{2,1,0:T(8,128)(2,1)} %param.11) | copy-start | bytes 98308
  0.6 13.9 %collective-permute-start = (bf16[128,2048]{1,0:T(8,128)(2,1)}, bf16[128,2048]{1,0:T(8,128)(2,1)S(1)}, u32[]{:S(2)}, u32[]{:S(2)}) collective-permute-start(bf16[128,2048]{1,0:T(8,128)(2,1)} %bitcast.310), channel_id=1, source_target_pairs={{0,16},{16,0},{1,17},{17,1},{2,18},{18,2},{3,19},{19,3},{4,20},{20... | collective-permute-start | bytes 1572872 | tf_op jit(solution)/shard_map/ppermute | solution.py:10
  14.6 3.4 %copy-start.4 = (bf16[128,2048]{1,0:T(8,128)(2,1)}, bf16[128,2048]{1,0:T(8,128)(2,1)S(1)}, u32[]{:S(2)}) copy-start(bf16[128,2048]{1,0:T(8,128)(2,1)S(1)} %collective-permute-done) | copy-start | bytes 1572868
  16.0 8.7 %copy-start.2 = (bf16[128,2048]{1,0:T(8,128)(2,1)}, bf16[128,2048]{1,0:T(8,128)(2,1)S(1)}, u32[]{:S(2)}) copy-start(bf16[128,2048]{1,0:T(8,128)(2,1)S(1)} %fusion.112) | copy-start | bytes 1572868
  16.0 8.6 %collective-permute-start.2 = (bf16[128,2048]{1,0:T(8,128)(2,1)S(1)}, bf16[128,2048]{1,0:T(8,128)(2,1)S(1)}, u32[]{:S(2)}, u32[]{:S(2)}) collective-permute-start(bf16[128,2048]{1,0:T(8,128)(2,1)S(1)} %fusion.112), channel_id=1, source_target_pairs={{1,0},{2,1},{3,2},{4,3},{5,4},{6,5},{7,6},{8,7},{9,8},{10,9},{11,1... | collective-permute-start | bytes 1572872 | tf_op jit(solution)/shard_map/ppermute | solution.py:16
  106.1 6.5 %copy-start.6 = (bf16[1,3,3,2048]{3,2,1,0:T(4,128)(2,1)S(1)}, bf16[1,3,3,2048]{3,2,1,0:T(4,128)(2,1)}, u32[]{:S(2)}) copy-start(bf16[1,3,3,2048]{3,2,1,0:T(4,128)(2,1)} %param.12) | copy-start | bytes 110596
  106.2 6.6 %copy-start.3 = (bf16[128,2048]{1,0:T(8,128)(2,1)S(1)}, bf16[128,2048]{1,0:T(8,128)(2,1)}, u32[]{:S(2)}) copy-start(bf16[128,2048]{1,0:T(8,128)(2,1)} %copy-done.2) | copy-start | bytes 1572868
  108.8 11.7 %collective-permute-start.1 = (bf16[128,2048]{1,0:T(8,128)(2,1)S(1)}, bf16[128,2048]{1,0:T(8,128)(2,1)}, u32[]{:S(2)}, u32[]{:S(2)}) collective-permute-start(bf16[128,2048]{1,0:T(8,128)(2,1)S(1)} %get-tuple-element.492), channel_id=1, source_target_pairs={{0,1},{1,2},{2,3},{3,4},{4,5},{5,6},{6,7},{7,8},{8,9},{9,10},{10,1... | collective-permute-start | bytes 1572872 | tf_op jit(solution)/shard_map/ppermute | solution.py:16
  301.9 4.3 %collective-permute-start.4 = (f32[128,128]{1,0:T(8,128)}, f32[128,128]{1,0:T(8,128)S(1)}, u32[]{:S(2)}, u32[]{:S(2)}) collective-permute-start(f32[128,128]{1,0:T(8,128)} %bitcast.13), channel_id=1, source_target_pairs={{0,1},{1,0},{2,3},{3,2},{4,5},{5,4},{6,7},{7,6},{8,9},{9,8},{10,11... | collective-permute-start | bytes 196616 | tf_op jit(solution)/shard_map/ppermute | solution.py:105
  302.0 1.5 copy-start
  302.0 1.5 copy-start.1
  303.8 7.7 %collective-permute-start.3 = (bf16[3,2,2048]{2,1,0:T(2,128)(2,1)S(1)}, bf16[3,2,2048]{2,1,0:T(2,128)(2,1)S(1)}, u32[]{:S(2)}, u32[]{:S(2)}) collective-permute-start(bf16[3,2,2048]{2,1,0:T(2,128)(2,1)S(1)} %slice.51), channel_id=1, source_target_pairs={{1,0},{2,1},{3,2},{4,3},{5,4},{6,5},{7,6},{8,7},{9,8},{10,9},{11,1... | collective-permute-start | bytes 73736 | tf_op jit(solution)/shard_map/ppermute | solution.py:16
  307.1 4.3 %collective-permute-start.5 = (f32[128,128]{1,0:T(8,128)S(1)}, f32[128,128]{1,0:T(8,128)S(1)}, u32[]{:S(2)}, u32[]{:S(2)}) collective-permute-start(f32[128,128]{1,0:T(8,128)S(1)} %bitcast_add_fusion), channel_id=1, source_target_pairs={{0,2},{1,3},{2,0},{3,1},{4,6},{5,7},{6,4},{7,5},{8,10},{9,11},{10,... | collective-permute-start | bytes 196616 | tf_op jit(solution)/shard_map/ppermute | solution.py:105
  311.4 4.3 %collective-permute-start.6 = (f32[128,128]{1,0:T(8,128)S(1)}, f32[128,128]{1,0:T(8,128)S(1)}, u32[]{:S(2)}, u32[]{:S(2)}) collective-permute-start(f32[128,128]{1,0:T(8,128)S(1)} %add.1045), channel_id=1, source_target_pairs={{0,4},{1,5},{2,6},{3,7},{4,0},{5,1},{6,2},{7,3},{8,12},{9,13},{10,... | collective-permute-start | bytes 196616 | tf_op jit(solution)/shard_map/ppermute | solution.py:105
  315.7 5.2 %collective-permute-start.7 = (f32[128,128]{1,0:T(8,128)S(1)}, f32[128,128]{1,0:T(8,128)S(1)}, u32[]{:S(2)}, u32[]{:S(2)}) collective-permute-start(f32[128,128]{1,0:T(8,128)S(1)} %add.1046), channel_id=1, source_target_pairs={{0,8},{1,9},{2,10},{3,11},{4,12},{5,13},{6,14},{7,15},{8,0},{9,1},... | collective-permute-start | bytes 196616 | tf_op jit(solution)/shard_map/ppermute | solution.py:105
